TPU v7x, 256 devices: a whole 4x4x8 slice. The times are simulated.
256 devices in a mesh: ctx: 128 (over z, x_lo, y, core), ch: 2 (over x_hi).
Axes of the slice: x: 4 (x_hi: 2, x_lo: 2; x = x_hi * 2 + x_lo), y: 4, z: 8, core: 2. Of those that a mesh axis runs over, the one named last changes fastest.
Arguments:
- query_proj: bfloat16 [32768, 2048], P('ctx', 'ch'), may hold values from -64 to 64
- key_proj: bfloat16 [32768, 2048], P('ctx', 'ch'), may hold values from -6 to 6
- value_proj: bfloat16 [32768, 2048], P('ctx', 'ch'), may hold values from -6 to 6
- filters: bfloat16 [1024, 2048], P('ctx', 'ch'), may hold values from -0.1875 to 0.1875
- cotangent: bfloat16 [32768, 2048], P('ctx', 'ch'), may hold values from -6 to 6
- stock_id: int32 [32768], P('ctx'), may hold values from 0 to 511
- stock_class: int32 [512], replicated, may hold values from 0 to 10
- cond_table: float32 [11, 2048], P(None, 'ch'), may hold values from -2.5 to 2.5
Outputs:
- normed_out: bfloat16 [32768, 2048], P('ctx', 'ch')
- grad_query: bfloat16 [32768, 2048], P('ctx', 'ch')
- grad_key: bfloat16 [32768, 2048], P('ctx', 'ch')
- grad_value: bfloat16 [32768, 2048], P('ctx', 'ch')
- grad_filter: float32 [1024, 2048], P('ctx', 'ch')
All inputs are finite; a program needn't handle non-finite values.
Results may differ from a plain program's by a relative error of at most 0.005.
Values may be sent and summed in bfloat16 or wider, within the bound.
No kernel may reach another device: no remote copies, remote signals or barrier semaphores. Data moves between devices by JAX's collectives and lax.ppermute only.
A program may use at most 128 MiB of HBM per device.

v0:
```python
import math
import jax
import jax.numpy as jnp
from jax import lax
from jax.sharding import PartitionSpec as P

REACH = 4
EPSILON = 1e-05
PRECISE = lax.Precision.HIGHEST
TRANSFORM = lax.Precision.HIGH


def from_behind(block, axis, distance):
    devices = range(lax.axis_size(axis))
    route = [(i - distance, i) for i in devices if i - distance in devices]
    return lax.ppermute(block, axis, route)


def product_tables(length, flipped):
    frequency = lax.broadcasted_iota(jnp.int32, (length, length), 0)
    position = lax.broadcasted_iota(jnp.int32, (length, length), 1)
    if flipped:
        position = length - 1 - position
    phase_index = (2 * frequency + 1) * position % (4 * length)
    angles = phase_index.astype(jnp.float32) * (math.pi / (2 * length))
    return (jnp.cos(angles), jnp.sin(angles))


def output_tables(length, flipped):
    position = lax.broadcasted_iota(jnp.int32, (length, length), 0)
    frequency = lax.broadcasted_iota(jnp.int32, (length, length), 1)
    if flipped:
        position = 2 * length - 1 - position
    else:
        position = length + position
    phase_index = (2 * frequency + 1) * position % (4 * length)
    angles = phase_index.astype(jnp.float32) * (math.pi / (2 * length))
    return (jnp.cos(angles) / length, jnp.sin(angles) / length)


def spectra(tables, pieces):
    cosine, sine_table = tables
    real_part = jnp.einsum("fs,nsc->fnc", cosine, pieces, precision=TRANSFORM)
    imag_part = -jnp.einsum("fs,nsc->fnc", sine_table, pieces, precision=TRANSFORM)
    return (real_part, imag_part)


def signals(tables, spectrum):
    cosine, sine_table = tables
    return jnp.einsum("tf,fnc->ntc", cosine, spectrum[0], precision=TRANSFORM) - jnp.einsum(
        "tf,fnc->ntc", sine_table, spectrum[1], precision=TRANSFORM
    )


def adjoint_spectra(tables, pieces):
    cosine, sine_table = tables
    real_part = jnp.einsum("tf,ntc->fnc", cosine, pieces, precision=TRANSFORM)
    imag_part = -jnp.einsum("tf,ntc->fnc", sine_table, pieces, precision=TRANSFORM)
    return (real_part, imag_part)


def complex_product(left_pair, right_pair):
    return (
        left_pair[0] * right_pair[0] - left_pair[1] * right_pair[1],
        left_pair[0] * right_pair[1] + left_pair[1] * right_pair[0],
    )


def complex_add(left_pair, right_pair):
    return (left_pair[0] + right_pair[0], left_pair[1] + right_pair[1])


def alternating(length):
    return jnp.where(jnp.arange(length) % 2 == 0, 1.0, -1.0).astype(jnp.float32)[:, None, None]


def filter_segments(tables, filter_full, length, reach_blocks):
    channels = filter_full.shape[1]
    lag_spectra = spectra(tables, filter_full.reshape(reach_blocks, length, channels))
    alternate = alternating(length)
    segments = []
    for distance in range(reach_blocks + 1):
        real_part = jnp.zeros((length, 1, channels), jnp.float32)
        imag_part = jnp.zeros((length, 1, channels), jnp.float32)
        if distance >= 1:
            real_part = lag_spectra[0][:, distance - 1 : distance]
            imag_part = lag_spectra[1][:, distance - 1 : distance]
        if distance < reach_blocks:
            real_part = real_part + alternate * lag_spectra[1][:, distance : distance + 1]
            imag_part = imag_part - alternate * lag_spectra[0][:, distance : distance + 1]
        segments.append((real_part, imag_part))
    return segments


def segment_grad(adjoint, spectrum):
    real_part = jnp.sum(adjoint[0] * spectrum[0] + adjoint[1] * spectrum[1], axis=1, keepdims=True)
    imag_part = jnp.sum(adjoint[1] * spectrum[0] - adjoint[0] * spectrum[1], axis=1, keepdims=True)
    return (real_part, imag_part)


def filter_gradient(tables, seg_grads, length, reach_blocks):
    alternate = alternating(length)
    grad_real = []
    grad_imag = []
    for lag_block in range(reach_blocks):
        grad_real.append(seg_grads[lag_block + 1][0] - alternate * seg_grads[lag_block][1])
        grad_imag.append(seg_grads[lag_block + 1][1] + alternate * seg_grads[lag_block][0])
    grad_real = jnp.concatenate(grad_real, axis=1)
    grad_imag = jnp.concatenate(grad_imag, axis=1)
    cosine, sine_table = tables
    lag_rows = jnp.einsum("fs,fmc->msc", cosine, grad_real, precision=TRANSFORM) - jnp.einsum(
        "fs,fmc->msc", sine_table, grad_imag, precision=TRANSFORM
    )
    return lag_rows.reshape(reach_blocks * length, lag_rows.shape[2])


def shards(query_proj, key_proj, value_proj, filters, cotangent, stock_id, stock_class, cond_table):
    length = key_proj.shape[0]
    local_channels = key_proj.shape[1]
    total_channels = local_channels * lax.axis_size("ch")
    forward_tables = product_tables(length, False)
    reverse_tables = product_tables(length, True)
    out_tables = output_tables(length, False)
    back_tables = output_tables(length, True)
    stock_hits = (
        stock_id[:, None] == jnp.arange(stock_class.shape[0], dtype=jnp.int32)[None, :]
    ).astype(jnp.float32)
    class_hits = (
        stock_class[:, None] == jnp.arange(cond_table.shape[0], dtype=jnp.int32)[None, :]
    ).astype(jnp.float32)
    event_class = jnp.dot(
        stock_hits, class_hits, precision=PRECISE, preferred_element_type=jnp.float32
    )
    cond_rows = jnp.dot(
        event_class, cond_table, precision=PRECISE, preferred_element_type=jnp.float32
    )
    gate_rows = query_proj.astype(jnp.float32) * (1.0 + cond_rows)
    mixed_in = (key_proj.astype(jnp.float32) * value_proj.astype(jnp.float32)).astype(jnp.bfloat16)
    filter_full = lax.all_gather(filters, "ctx", axis=0, tiled=True).astype(jnp.float32)
    segments = filter_segments(forward_tables, filter_full, length, REACH)
    neighbours = [spectra(forward_tables, mixed_in.astype(jnp.float32)[None])]
    moving = mixed_in
    for distance in range(1, REACH + 1):
        moving = from_behind(moving, "ctx", 1)
        neighbours.append(spectra(forward_tables, moving.astype(jnp.float32)[None]))
    accumulated = complex_product(segments[0], neighbours[0])
    for distance in range(1, REACH + 1):
        accumulated = complex_add(
            accumulated, complex_product(segments[distance], neighbours[distance])
        )
    conv_out = signals(out_tables, accumulated)[0]
    scaled = gate_rows * conv_out
    squares = lax.psum(jnp.sum(scaled * scaled, axis=1), "ch")
    inv_rms = lax.rsqrt(squares / total_channels + EPSILON)[:, None]
    normed = scaled * inv_rms
    normed_out = normed.astype(jnp.bfloat16)
    upstream = cotangent.astype(jnp.float32)
    inner_sum = lax.psum(jnp.sum(upstream * normed, axis=1), "ch")
    grad_scaled = inv_rms * (upstream - normed * (inner_sum / total_channels)[:, None])
    grad_query = (grad_scaled * conv_out * (1.0 + cond_rows)).astype(jnp.bfloat16)
    grad_conv = (grad_scaled * gate_rows).astype(jnp.bfloat16)
    own_reverse = spectra(reverse_tables, grad_conv.astype(jnp.float32)[None])
    accumulated = complex_product(segments[0], own_reverse)
    moving = grad_conv
    for distance in range(1, REACH + 1):
        moving = from_behind(moving, "ctx", -1)
        later_spec = spectra(reverse_tables, moving.astype(jnp.float32)[None])
        accumulated = complex_add(accumulated, complex_product(segments[distance], later_spec))
    grad_mixed = signals(back_tables, accumulated)[0]
    adjoint = adjoint_spectra(out_tables, grad_conv.astype(jnp.float32)[None])
    seg_grads = [segment_grad(adjoint, neighbours[distance]) for distance in range(REACH + 1)]
    filter_term = filter_gradient(forward_tables, seg_grads, length, REACH)
    grad_filter = lax.psum_scatter(filter_term, "ctx", scatter_dimension=0, tiled=True)
    grad_key = (grad_mixed * value_proj.astype(jnp.float32)).astype(jnp.bfloat16)
    grad_value = (grad_mixed * key_proj.astype(jnp.float32)).astype(jnp.bfloat16)
    return (normed_out, grad_query, grad_key, grad_value, grad_filter)


def solution(mesh):
    return jax.shard_map(
        shards,
        mesh=mesh,
        in_specs=(
            P("ctx", "ch"),
            P("ctx", "ch"),
            P("ctx", "ch"),
            P("ctx", "ch"),
            P("ctx", "ch"),
            P("ctx"),
            P(),
            P(None, "ch"),
        ),
        out_specs=(P("ctx", "ch"), P("ctx", "ch"), P("ctx", "ch"), P("ctx", "ch"), P("ctx", "ch")),
        check_vma=False,
    )
```

profile of v0, /device:TPU:4, one launch (start us, length us, event | category | flops | bytes accessed | tf_op | source)
XLA Modules:
  0.0 859.0 jit_solution(3938443588100111600)
XLA Ops:
  9.2 1.4 copy.15
  10.8 1.8 collective-permute-start
  13.7 2.0 convolution_add_fusion
  15.6 2.7 fusion.209
  18.3 2.7 fusion.222
  21.0 3.8 collective-permute-start.1
  24.7 2.7 fusion.207
  27.4 2.7 fusion.219
  30.1 2.8 collective-permute-start.2
  32.9 2.0 fusion.205
  34.9 1.9 fusion.217
  36.9 6.6 collective-permute-start.3
  43.4 2.1 fusion.203
  45.6 2.7 fusion.215
  48.2 2.7 fusion.201
  50.9 2.6 fusion.213
  53.5 172.6 %all-gather.2.cloned.1.call-done = bf16[1024,1024]{1,0:T(8,128)(2,1)} async-done(((bf16[8,1024]{1,0:T(8,128)(2,1)}), bf16[1024,1024]{1,0:T(8,128)(2,1)}) %all-gather.2.cloned.1.call-update) | async-done | bytes 2097168 | tf_op jit(solution)/shard_map/all_gather | solution.py:139
  226.1 4.0 convolution_negate_fusion
  230.3 2.3 fusion.172
  236.0 3.8 fusion.35
  239.9 4.9 multiply_reduce_fusion
  244.8 6.4 psum.14
  251.2 1.7 fusion.29
  252.9 6.5 psum.15
  259.4 3.7 multiply_convert_fusion
  263.1 1.4 fusion.184
  264.5 1.4 fusion.185
  268.2 1.6 add_bitcast_fusion.3
  270.0 3.8 fusion
  273.9 6.1 fusion.16
  282.3 2.5 collective-permute-done.4
  286.1 8.4 collective-permute-done.5
  295.8 1.5 convolution_bitcast_fusion.4
  297.2 1.5 fusion.23
  298.7 1.5 convolution_bitcast_fusion.3
  300.2 1.5 fusion.22
  301.7 3.6 collective-permute-done.6
  305.3 1.5 collective-permute-start.7
  306.8 1.5 convolution_bitcast_fusion.2
  308.3 1.5 fusion.21
  309.8 1.5 convolution_bitcast_fusion.1
  311.3 1.5 fusion.20
  312.8 3.1 collective-permute-done.7
  315.9 1.5 convolution_bitcast_fusion
  317.4 1.5 fusion.19
  318.9 3.3 fusion.32
  322.2 3.6 fusion.26
  327.9 524.0 %reduce-scatter.2.cloned.1.call-done = f32[8,1024]{1,0:T(8,128)} async-done(((f32[1024,1024]{1,0:T(8,128)}), f32[8,1024]{1,0:T(8,128)}) %reduce-scatter.2.cloned.1.call-update) | async-done | bytes 32784 | tf_op jit(solution)/shard_map/reduce_scatter | solution.py:173
  (82 shorter events, 16.0 us)
Async XLA Ops:
  7.2 6.5 copy-start
  7.2 219.0 %all-gather.2.cloned.1.call-start = ((), (), s32[]{:S(2)}) async-start(), calls=%async_computation.1 | async-start | bytes 2113536 | tf_op jit(solution)/shard_map/all_gather | solution.py:139
  7.9 844.0 %reduce-scatter.2.cloned.1.call-start = ((), (), s32[]{:S(2)}) async-start(), calls=%async_computation.2 | async-start | bytes 4227072 | tf_op jit(solution)/shard_map/reduce_scatter | solution.py:173
  9.2 18.2 %copy-start.22 = (bf16[256,1024]{0,1:T(8,128)(2,1)}, bf16[256,1024]{0,1:T(8,128)(2,1)S(1)}, u32[]{:S(2)}) copy-start(bf16[256,1024]{0,1:T(8,128)(2,1)S(1)} %copy.14) | copy-start | bytes 1572868
  10.7 19.4 %copy-start.24 = (bf16[256,1024]{0,1:T(8,128)(2,1)}, bf16[256,1024]{0,1:T(8,128)(2,1)S(1)}, u32[]{:S(2)}) copy-start(bf16[256,1024]{0,1:T(8,128)(2,1)S(1)} %copy.15) | copy-start | bytes 1572868
  10.8 10.2 %collective-permute-start = (bf16[256,1024]{0,1:T(8,128)(2,1)S(1)}, bf16[256,1024]{0,1:T(8,128)(2,1)S(1)}, u32[]{:S(2)}, u32[]{:S(2)}) collective-permute-start(bf16[256,1024]{0,1:T(8,128)(2,1)S(1)} %fusion.27), channel_id=1, source_target_pairs={{0,2},{2,4},{4,6},{6,8},{8,10},{10,12},{12,14},{14,16},{16,18},{18... | collective-permute-start | bytes 1572872 | tf_op jit(solution)/shard_map/ppermute | solution.py:16
  21.0 9.1 %collective-permute-start.1 = (bf16[256,1024]{0,1:T(8,128)(2,1)S(1)}, bf16[256,1024]{0,1:T(8,128)(2,1)S(1)}, u32[]{:S(2)}, u32[]{:S(2)}) collective-permute-start(bf16[256,1024]{0,1:T(8,128)(2,1)S(1)} %collective-permute-done), channel_id=1, source_target_pairs={{0,2},{2,4},{4,6},{6,8},{8,10},{10,12},{12,14},{14,16},{16,18},{18... | collective-permute-start | bytes 1572872 | tf_op jit(solution)/shard_map/ppermute | solution.py:16
  30.1 6.8 collective-permute-start.2
  36.9 11.4 %collective-permute-start.3 = (bf16[256,1024]{0,1:T(8,128)(2,1)S(1)}, bf16[256,1024]{0,1:T(8,128)(2,1)S(1)}, u32[]{:S(2)}, u32[]{:S(2)}) collective-permute-start(bf16[256,1024]{0,1:T(8,128)(2,1)S(1)} %collective-permute-done.2), channel_id=1, source_target_pairs={{0,2},{2,4},{4,6},{6,8},{8,10},{10,12},{12,14},{14,16},{16,18},{18... | collective-permute-start | bytes 1572872 | tf_op jit(solution)/shard_map/ppermute | solution.py:16
  226.1 4.1 copy-start.21
  226.1 6.5 copy-start.18
  230.2 9.6 %copy-start.8 = (f32[256,4,1024]{2,0,1:T(8,128)}, f32[256,4,1024]{2,0,1:T(8,128)S(1)}, u32[]{:S(2)}) copy-start(f32[256,4,1024]{2,0,1:T(8,128)S(1)} %convolution_negate_fusion) | copy-start | bytes 12582916
  230.2 2.4 copy-start.2
  230.2 3.0 copy-start.4
  230.2 3.5 copy-start.6
  230.2 4.6 copy-start.12
  230.3 5.5 copy-start.14
  230.3 5.8 copy-start.16
  232.6 7.3 copy-start.10
  236.0 3.8 copy-start.20
  236.0 3.8 copy-start.26
  259.4 6.6 copy-start.3
  259.4 6.6 copy-start.5
  259.4 6.6 copy-start.7
  263.1 4.1 copy-start.27
  266.0 1.2 copy-start.13
  266.0 1.5 copy-start.15
  266.0 1.8 copy-start.17
  266.0 2.1 copy-start.19
  280.0 1.0 copy-start.28
  281.0 3.8 collective-permute-start.4
  284.8 9.7 %collective-permute-start.5 = (bf16[256,1024]{1,0:T(8,128)(2,1)S(1)}, bf16[256,1024]{1,0:T(8,128)(2,1)S(1)}, u32[]{:S(2)}, u32[]{:S(2)}) collective-permute-start(bf16[256,1024]{1,0:T(8,128)(2,1)S(1)} %collective-permute-done.4), channel_id=1, source_target_pairs={{2,0},{4,2},{6,4},{8,6},{10,8},{12,10},{14,12},{16,14},{18,16},{20... | collective-permute-start | bytes 1572872 | tf_op jit(solution)/shard_map/ppermute | solution.py:16
  294.5 10.8 %collective-permute-start.6 = (bf16[256,1024]{1,0:T(8,128)(2,1)S(1)}, bf16[256,1024]{1,0:T(8,128)(2,1)S(1)}, u32[]{:S(2)}, u32[]{:S(2)}) collective-permute-start(bf16[256,1024]{1,0:T(8,128)(2,1)S(1)} %collective-permute-done.5), channel_id=1, source_target_pairs={{2,0},{4,2},{6,4},{8,6},{10,8},{12,10},{14,12},{16,14},{18,16},{20... | collective-permute-start | bytes 1572872 | tf_op jit(solution)/shard_map/ppermute | solution.py:16
  305.3 10.6 %collective-permute-start.7 = (bf16[256,1024]{1,0:T(8,128)(2,1)S(1)}, bf16[256,1024]{1,0:T(8,128)(2,1)S(1)}, u32[]{:S(2)}, u32[]{:S(2)}) collective-permute-start(bf16[256,1024]{1,0:T(8,128)(2,1)S(1)} %collective-permute-done.6), channel_id=1, source_target_pairs={{2,0},{4,2},{6,4},{8,6},{10,8},{12,10},{14,12},{16,14},{18,16},{20... | collective-permute-start | bytes 1572872 | tf_op jit(solution)/shard_map/ppermute | solution.py:16
  308.3 10.6 %copy-start.9 = (f32[256,4,1024]{2,0,1:T(8,128)S(1)}, f32[256,4,1024]{2,0,1:T(8,128)}, u32[]{:S(2)}) copy-start(f32[256,4,1024]{2,0,1:T(8,128)} %copy-done.8) | copy-start | bytes 12582916
  308.3 10.6 %copy-start.11 = (f32[256,4,1024]{2,0,1:T(8,128)S(1)}, f32[256,4,1024]{2,0,1:T(8,128)}, u32[]{:S(2)}) copy-start(f32[256,4,1024]{2,0,1:T(8,128)} %copy-done.10) | copy-start | bytes 12582916
  318.9 3.3 copy-start.23
  318.9 3.3 copy-start.25
  322.2 529.7 %copy-start.1 = (f32[11,1024]{1,0:T(8,128)S(1)}, f32[11,1024]{1,0:T(8,128)}, u32[]{:S(2)}) copy-start(f32[11,1024]{1,0:T(8,128)} %param.15) | copy-start | bytes 135172
Sparse Core Ops, SparseCore 0:
  9.9 216.2 all-gather.1
  280.1 571.7 reduce-scatter.1
where the time goes:
time: 868 us; the launch traced here: 859 us
  waiting for transfers between devices  715 us (82%)
  matrix products  77.2 us (9%)
  starting transfers between devices  20.3 us (2%)
  between operations  14.9 us (2%)
  blocking collectives  12.9 us (1%)
  local copies, waits for them, and re-layouts  10.2 us (1%)
    reduce_scatter x1, waiting for transfers between devices, shards(): lax.psum_scatter(filter_term, 'ctx', scatter_dimension=0, tiled=True)  524 us
    all_gather x1, waiting for transfers between devices, shards(): lax.all_gather(filters, 'ctx', axis=0, tiled=True).astype(jnp.float32)  173 us
    dot_general x11, matrix products, spectra(): jnp.einsum('fs,nsc->fnc', sine_table, pieces, precision=TRANSFORM)  23.5 us
    dot_general x11, matrix products, spectra(): real_part = jnp.einsum('fs,nsc->fnc', cosine, pieces, precision=TRANSFORM)  22.3 us
    ppermute x8, starting transfers between devices, from_behind(): return lax.ppermute(block, axis, route)  20.3 us
    ppermute x8, waiting for transfers between devices, from_behind(): return lax.ppermute(block, axis, route)  17.5 us
  transfers between devices with their start and end apart: 10, of which 6 were waited for; matrix products, arithmetic and copies ran while one was open for 6% of the time, Pallas kernels for 0%

commit v1 on v0

--- a/solution.py
+++ b/solution.py
@@ -136,7 +136,9 @@
     )
     gate_rows = query_proj.astype(jnp.float32) * (1.0 + cond_rows)
     mixed_in = (key_proj.astype(jnp.float32) * value_proj.astype(jnp.float32)).astype(jnp.bfloat16)
-    filter_full = lax.all_gather(filters, "ctx", axis=0, tiled=True).astype(jnp.float32)
+    filter_full = jnp.concatenate(
+        lax.all_to_all(jnp.stack([filters] * lax.axis_size("ctx")), "ctx", 0, 0), axis=0
+    ).astype(jnp.float32)
     segments = filter_segments(forward_tables, filter_full, length, REACH)
     neighbours = [spectra(forward_tables, mixed_in.astype(jnp.float32)[None])]
     moving = mixed_in

time: 868 us -> 764 us (0.88)
  waiting for transfers between devices: 715 us -> 584 us
  starting transfers between devices: 20.3 us -> 47.9 us
    all_gather x1 -> x0, waiting for transfers between devices: 173 us -> none  [shards(): lax.all_gather(filters, 'ctx', axis=0, tiled=True).astype(jnp.float32)]
    reduce_scatter x1, waiting for transfers between devices: 524 us -> 562 us  [shards(): lax.psum_scatter(filter_term, 'ctx', scatter_dimension=0, tiled=True)]
    all_to_all x0 -> x1, starting transfers between devices: none -> 14.6 us  [shards(): lax.all_to_all(jnp.stack([filters] * lax.axis_size('ctx')), 'ctx', 0, 0)]
    ppermute x8, starting transfers between devices: 20.3 us -> 33.3 us  [from_behind(): return lax.ppermute(block, axis, route)]
  transfers between devices with their start and end apart: 10 -> 10, of which waited for: 6 -> 5; matrix products, arithmetic and copies ran while one was open for 6% -> 7% of each run, Pallas kernels for 0% -> 0%
where the time goes in v1:
time: 764 us; the launch traced here: 755 us
  waiting for transfers between devices  584 us (76%)
  matrix products  79.4 us (10%)
  starting transfers between devices  47.9 us (6%)
  between operations  15 us (2%)
  blocking collectives  12.9 us (2%)
  other arithmetic  8.64 us (1%)
    reduce_scatter x1, waiting for transfers between devices, shards(): lax.psum_scatter(filter_term, 'ctx', scatter_dimension=0, tiled=True)  562 us
    ppermute x8, starting transfers between devices, from_behind(): return lax.ppermute(block, axis, route)  33.3 us
    dot_general x11, matrix products, spectra(): real_part = jnp.einsum('fs,nsc->fnc', cosine, pieces, precision=TRANSFORM)  25.4 us
    dot_general x11, matrix products, spectra(): jnp.einsum('fs,nsc->fnc', sine_table, pieces, precision=TRANSFORM)  23.3 us
    ppermute x8, waiting for transfers between devices, from_behind(): return lax.ppermute(block, axis, route)  22.7 us
  transfers between devices with their start and end apart: 10, of which 5 were waited for; matrix products, arithmetic and copies ran while one was open for 7% of the time, Pallas kernels for 0%

profile of v1, /device:TPU:4, one launch (start us, length us, event | category | flops | bytes accessed | tf_op | source)
XLA Modules:
  0.0 755.2 jit_solution(4797553325605524892)
XLA Ops:
  7.2 2.4 stack.2
  9.6 14.6 %all-to-all-start = ((bf16[128,8,1024]{2,1,0:T(8,128)(2,1)}), bf16[128,8,1024]{2,1,0:T(8,128)(2,1)}, u32[]{:S(2)}, u32[]{:S(2)}) async-start(bf16[128,8,1024]{2,1,0:T(8,128)(2,1)} %stack.2), calls=%async_computation | async-start | bytes 4194304 | tf_op jit(solution)/shard_map/all_to_all | solution.py:140
  24.9 1.5 collective-permute-start
  26.8 2.0 convolution_add_fusion
  28.7 2.7 fusion.209
  31.4 2.7 fusion.222
  34.1 5.6 collective-permute-start.1
  39.7 2.7 fusion.207
  42.4 2.7 fusion.219
  45.1 10.5 %collective-permute-start.2 = (bf16[256,1024]{0,1:T(8,128)(2,1)S(1)}, bf16[256,1024]{0,1:T(8,128)(2,1)S(1)}, u32[]{:S(2)}, u32[]{:S(2)}) collective-permute-start(bf16[256,1024]{0,1:T(8,128)(2,1)S(1)} %collective-permute-done.1), channel_id=1, source_target_pairs={{0,2},{2,4},{4,6},{6,8},{8,10},{10,12},{12,14},{14,16},{16,18},{18... | collective-permute-start | bytes 1572872 | tf_op jit(solution)/shard_map/ppermute | solution.py:16
  55.6 2.0 fusion.205
  57.5 1.9 fusion.217
  59.5 10.3 %collective-permute-start.3 = (bf16[256,1024]{0,1:T(8,128)(2,1)S(1)}, bf16[256,1024]{0,1:T(8,128)(2,1)S(1)}, u32[]{:S(2)}, u32[]{:S(2)}) collective-permute-start(bf16[256,1024]{0,1:T(8,128)(2,1)S(1)} %collective-permute-done.2), channel_id=1, source_target_pairs={{0,2},{2,4},{4,6},{6,8},{8,10},{10,12},{12,14},{14,16},{16,18},{18... | collective-permute-start | bytes 1572872 | tf_op jit(solution)/shard_map/ppermute | solution.py:16
  69.8 2.0 fusion.203
  71.8 2.7 fusion.215
  74.5 2.7 fusion.201
  77.1 2.6 fusion.213
  79.8 4.0 convolution_negate_fusion
  83.8 5.4 fusion.172
  89.4 3.8 fusion.35
  93.2 4.9 multiply_reduce_fusion
  98.1 6.4 psum.14
  104.5 1.7 fusion.29
  106.2 6.5 psum.15
  112.7 3.7 multiply_convert_fusion
  116.4 1.4 fusion.184
  117.9 1.4 fusion.185
  121.5 1.6 add_bitcast_fusion.3
  123.4 3.8 fusion
  127.2 6.1 fusion.16
  135.6 4.3 collective-permute-done.4
  141.2 12.2 %collective-permute-done.5 = bf16[256,1024]{1,0:T(8,128)(2,1)S(1)} collective-permute-done((bf16[256,1024]{1,0:T(8,128)(2,1)S(1)}, bf16[256,1024]{1,0:T(8,128)(2,1)S(1)}, u32[]{:S(2)}, u32[]{:S(2)}) %collective-permute-start.5) | collective-permute-done | bytes 524320 | tf_op jit(solution)/shard_map/ppermute | solution.py:16
  154.7 1.5 convolution_bitcast_fusion.4
  156.2 1.5 fusion.23
  157.7 1.5 convolution_bitcast_fusion.3
  159.2 1.5 fusion.22
  160.7 3.2 collective-permute-done.6
  163.9 1.5 collective-permute-start.7
  165.4 1.5 convolution_bitcast_fusion.2
  166.9 1.5 fusion.21
  168.4 1.5 convolution_bitcast_fusion.1
  169.9 1.5 fusion.20
  171.4 3.0 collective-permute-done.7
  174.4 1.5 convolution_bitcast_fusion
  175.9 1.5 fusion.19
  177.4 3.3 fusion.32
  180.7 3.6 fusion.26
  186.4 561.7 %reduce-scatter.2.cloned.1.call-done = f32[8,1024]{1,0:T(8,128)} async-done(((f32[1024,1024]{1,0:T(8,128)}), f32[8,1024]{1,0:T(8,128)}) %reduce-scatter.2.cloned.1.call-update) | async-done | bytes 32784 | tf_op jit(solution)/shard_map/reduce_scatter | solution.py:175
  (88 shorter events, 10.4 us)
Async XLA Ops:
  7.2 19.6 %copy-start = (f32[11,1024]{1,0:T(8,128)S(1)}, f32[11,1024]{1,0:T(8,128)}, u32[]{:S(2)}) copy-start(f32[11,1024]{1,0:T(8,128)} %param.15) | copy-start | bytes 135172
  7.2 17.1 %copy-start.28 = (bf16[256,1024]{1,0:T(8,128)(2,1)S(1)}, bf16[256,1024]{1,0:T(8,128)(2,1)}, u32[]{:S(2)}) copy-start(bf16[256,1024]{1,0:T(8,128)(2,1)} %param.9) | copy-start | bytes 1572868
  7.2 17.3 %copy-start.29 = (bf16[256,1024]{1,0:T(8,128)(2,1)S(1)}, bf16[256,1024]{1,0:T(8,128)(2,1)}, u32[]{:S(2)}) copy-start(bf16[256,1024]{1,0:T(8,128)(2,1)} %param.10) | copy-start | bytes 1572868
  9.6 16.8 %copy-start.30 = (s32[512]{0:T(512)S(1)}, s32[512]{0:T(512)}, u32[]{:S(2)}) copy-start(s32[512]{0:T(512)} %param.14) | copy-start | bytes 6148
  9.6 16.8 %copy-start.31 = (s32[256]{0:T(256)S(1)}, s32[256]{0:T(256)}, u32[]{:S(2)}) copy-start(s32[256]{0:T(256)} %param.13) | copy-start | bytes 3076
  9.6 70.1 %all-to-all-start = ((bf16[128,8,1024]{2,1,0:T(8,128)(2,1)}), bf16[128,8,1024]{2,1,0:T(8,128)(2,1)}, u32[]{:S(2)}, u32[]{:S(2)}) async-start(bf16[128,8,1024]{2,1,0:T(8,128)(2,1)} %stack.2), calls=%async_computation | async-start | bytes 4194304 | tf_op jit(solution)/shard_map/all_to_all | solution.py:140
  24.2 723.8 %reduce-scatter.2.cloned.1.call-start = ((), (), s32[]{:S(2)}) async-start(), calls=%async_computation.2 | async-start | bytes 4227072 | tf_op jit(solution)/shard_map/reduce_scatter | solution.py:175
  24.5 17.9 %copy-start.21 = (bf16[256,1024]{0,1:T(8,128)(2,1)}, bf16[256,1024]{0,1:T(8,128)(2,1)S(1)}, u32[]{:S(2)}) copy-start(bf16[256,1024]{0,1:T(8,128)(2,1)S(1)} %copy.14) | copy-start | bytes 1572868
  24.7 20.3 %copy-start.23 = (bf16[256,1024]{0,1:T(8,128)(2,1)}, bf16[256,1024]{0,1:T(8,128)(2,1)S(1)}, u32[]{:S(2)}) copy-start(bf16[256,1024]{0,1:T(8,128)(2,1)S(1)} %copy.15) | copy-start | bytes 1572868
  24.9 9.2 %collective-permute-start = (bf16[256,1024]{0,1:T(8,128)(2,1)S(1)}, bf16[256,1024]{0,1:T(8,128)(2,1)S(1)}, u32[]{:S(2)}, u32[]{:S(2)}) collective-permute-start(bf16[256,1024]{0,1:T(8,128)(2,1)S(1)} %fusion.27), channel_id=1, source_target_pairs={{0,2},{2,4},{4,6},{6,8},{8,10},{10,12},{12,14},{14,16},{16,18},{18... | collective-permute-start | bytes 1572872 | tf_op jit(solution)/shard_map/ppermute | solution.py:16
  34.1 11.0 %collective-permute-start.1 = (bf16[256,1024]{0,1:T(8,128)(2,1)S(1)}, bf16[256,1024]{0,1:T(8,128)(2,1)S(1)}, u32[]{:S(2)}, u32[]{:S(2)}) collective-permute-start(bf16[256,1024]{0,1:T(8,128)(2,1)S(1)} %collective-permute-done), channel_id=1, source_target_pairs={{0,2},{2,4},{4,6},{6,8},{8,10},{10,12},{12,14},{14,16},{16,18},{18... | collective-permute-start | bytes 1572872 | tf_op jit(solution)/shard_map/ppermute | solution.py:16
  45.1 14.4 %collective-permute-start.2 = (bf16[256,1024]{0,1:T(8,128)(2,1)S(1)}, bf16[256,1024]{0,1:T(8,128)(2,1)S(1)}, u32[]{:S(2)}, u32[]{:S(2)}) collective-permute-start(bf16[256,1024]{0,1:T(8,128)(2,1)S(1)} %collective-permute-done.1), channel_id=1, source_target_pairs={{0,2},{2,4},{4,6},{6,8},{8,10},{10,12},{12,14},{14,16},{16,18},{18... | collective-permute-start | bytes 1572872 | tf_op jit(solution)/shard_map/ppermute | solution.py:16
  59.5 15.0 %collective-permute-start.3 = (bf16[256,1024]{0,1:T(8,128)(2,1)S(1)}, bf16[256,1024]{0,1:T(8,128)(2,1)S(1)}, u32[]{:S(2)}, u32[]{:S(2)}) collective-permute-start(bf16[256,1024]{0,1:T(8,128)(2,1)S(1)} %collective-permute-done.2), channel_id=1, source_target_pairs={{0,2},{2,4},{4,6},{6,8},{8,10},{10,12},{12,14},{14,16},{16,18},{18... | collective-permute-start | bytes 1572872 | tf_op jit(solution)/shard_map/ppermute | solution.py:16
  79.8 9.5 %copy-start.18 = (f32[256,1024]{1,0:T(8,128)S(1)}, f32[256,1024]{1,0:T(8,128)}, u32[]{:S(2)}) copy-start(f32[256,1024]{1,0:T(8,128)} %fusion.219) | copy-start | bytes 3145732
  83.8 9.4 %copy-start.8 = (f32[256,4,1024]{2,0,1:T(8,128)}, f32[256,4,1024]{2,0,1:T(8,128)S(1)}, u32[]{:S(2)}) copy-start(f32[256,4,1024]{2,0,1:T(8,128)S(1)} %convolution_negate_fusion) | copy-start | bytes 12582916
  83.8 5.5 copy-start.2
  83.8 5.5 copy-start.4
  83.8 5.5 copy-start.6
  83.8 5.5 copy-start.12
  83.8 5.5 copy-start.14
  83.8 5.5 copy-start.16
  89.3 3.9 copy-start.10
  89.3 3.8 copy-start.20
  89.3 3.8 copy-start.25
  112.7 6.6 copy-start.3
  112.7 6.6 copy-start.5
  112.7 6.6 copy-start.7
  116.4 1.4 copy-start.26
  119.3 1.3 copy-start.13
  119.3 1.5 copy-start.15
  119.4 1.8 copy-start.17
  119.4 2.1 copy-start.19
  133.3 1.0 copy-start.27
  134.3 5.5 collective-permute-start.4
  139.9 13.5 %collective-permute-start.5 = (bf16[256,1024]{1,0:T(8,128)(2,1)S(1)}, bf16[256,1024]{1,0:T(8,128)(2,1)S(1)}, u32[]{:S(2)}, u32[]{:S(2)}) collective-permute-start(bf16[256,1024]{1,0:T(8,128)(2,1)S(1)} %collective-permute-done.4), channel_id=1, source_target_pairs={{2,0},{4,2},{6,4},{8,6},{10,8},{12,10},{14,12},{16,14},{18,16},{20... | collective-permute-start | bytes 1572872 | tf_op jit(solution)/shard_map/ppermute | solution.py:16
  153.4 10.5 %collective-permute-start.6 = (bf16[256,1024]{1,0:T(8,128)(2,1)S(1)}, bf16[256,1024]{1,0:T(8,128)(2,1)S(1)}, u32[]{:S(2)}, u32[]{:S(2)}) collective-permute-start(bf16[256,1024]{1,0:T(8,128)(2,1)S(1)} %collective-permute-done.5), channel_id=1, source_target_pairs={{2,0},{4,2},{6,4},{8,6},{10,8},{12,10},{14,12},{16,14},{18,16},{20... | collective-permute-start | bytes 1572872 | tf_op jit(solution)/shard_map/ppermute | solution.py:16
  163.9 10.5 %collective-permute-start.7 = (bf16[256,1024]{1,0:T(8,128)(2,1)S(1)}, bf16[256,1024]{1,0:T(8,128)(2,1)S(1)}, u32[]{:S(2)}, u32[]{:S(2)}) collective-permute-start(bf16[256,1024]{1,0:T(8,128)(2,1)S(1)} %collective-permute-done.6), channel_id=1, source_target_pairs={{2,0},{4,2},{6,4},{8,6},{10,8},{12,10},{14,12},{16,14},{18,16},{20... | collective-permute-start | bytes 1572872 | tf_op jit(solution)/shard_map/ppermute | solution.py:16
  166.9 10.5 %copy-start.9 = (f32[256,4,1024]{2,0,1:T(8,128)S(1)}, f32[256,4,1024]{2,0,1:T(8,128)}, u32[]{:S(2)}) copy-start(f32[256,4,1024]{2,0,1:T(8,128)} %copy-done.8) | copy-start | bytes 12582916
  166.9 10.5 %copy-start.11 = (f32[256,4,1024]{2,0,1:T(8,128)S(1)}, f32[256,4,1024]{2,0,1:T(8,128)}, u32[]{:S(2)}) copy-start(f32[256,4,1024]{2,0,1:T(8,128)} %copy-done.10) | copy-start | bytes 12582916
  177.4 3.3 copy-start.22
  177.4 3.3 copy-start.24
  180.7 567.3 %copy-start.1 = (f32[11,1024]{1,0:T(8,128)S(1)}, f32[11,1024]{1,0:T(8,128)}, u32[]{:S(2)}) copy-start(f32[11,1024]{1,0:T(8,128)} %param.15) | copy-start | bytes 135172
Sparse Core Ops, SparseCore 0:
  133.4 614.5 reduce-scatter.1
